TPU v7x, 128 devices: a whole 4x4x4 slice. The times are simulated.
128 devices in a mesh: seq: 8 (over z, core), tp: 16 (over x, y).
Axes of the slice: x: 4, y: 4, z: 4, core: 2. Of those that a mesh axis runs over, the one named last changes fastest.
Arguments:
- sequence_in: bfloat16 [1536, 4096], P('tp', 'seq')
- conv_weight: bfloat16 [3, 1536, 3, 1536], P(None, 'tp')
- norm_gain: float32 [3, 1536], P(None, 'tp'), may hold values from 0.1 to 1.9
- tissue_scale: float32 [367, 1536], replicated, may hold values from 0.3 to 3
- donor_offset: int32 [2048], P('seq'), may hold values from 0 to 511
- acceptor_owner: int32 [2048, 1], P('seq'), may hold values from 0 to 7; in each aligned block of 256 rows (0 to 255, 256 to 511, ...) at most 128 rows name the same one
- acceptor_offset: int32 [2048], P('seq'), may hold values from 0 to 511
- tissue: int32 [2048], P('seq'), may hold values from 0 to 366
- tower_grad: float32 [1536, 4096], P('tp', 'seq'), may hold values from -6 to 6
- score_grad: float32 [2048], P('seq'), may hold values from -24 to 24
Outputs:
- scores: float32 [2048], P('seq')
- input_grad: float32 [1536, 4096], P('tp', 'seq')
- weight_grad: float32 [3, 1536, 3, 1536], P(None, 'tp')
- gain_grad: float32 [3, 1536], P(None, 'tp')
Inputs may be any that keep to these rules, and one draw needn't show every extreme that they name: `acceptor_owner`: among the 256 junctions of one index of seq, at most 128 have their acceptor on one index of seq.
All inputs are finite; a program needn't handle non-finite values.
Results may differ from a plain program's by a relative error of at most 0.025.
Values may be sent and summed in bfloat16 or wider, within the bound.
A program may use at most 128 MiB of HBM per device.

v0:
```python
import math
import jax
import jax.numpy as jnp
from jax import lax
from jax.sharding import PartitionSpec as P

CHANNELS = 1536
LAYERS = 3
CAP = 128
EPSILON = 1e-06


def with_halo(x, sides, width):
    for axis, dim in sides:
        count, length = (lax.axis_size(axis), x.shape[dim])
        up = [(i, (i + 1) % count) for i in range(count - 1)]
        down = [(j, i) for i, j in up]
        last = lax.slice_in_dim(x, length - width, length, axis=dim)
        initial = lax.slice_in_dim(x, 0, width, axis=dim)
        before = lax.ppermute(last, axis, up)
        after = lax.ppermute(initial, axis, down)
        x = jnp.concatenate([before, x, after], axis=dim)
    return x


def gelu_fn(value):
    return jax.nn.gelu(value, approximate=True)


def widen(block, width):
    return with_halo(block, (("seq", 1),), width)


def forward_taps(weights, padded, reach, length):
    total = jnp.zeros((weights.shape[0], length), jnp.float32)
    for tap in range(3):
        total = total + jnp.dot(
            weights[:, tap, :],
            padded[:, tap * reach : tap * reach + length],
            preferred_element_type=jnp.float32,
        )
    return total


def backward_taps(weights, grad_pad, reach, length):
    total = jnp.zeros((weights.shape[2], length), jnp.float32)
    for tap in range(3):
        total = total + lax.dot_general(
            weights[:, tap, :],
            grad_pad[:, (2 - tap) * reach : (2 - tap) * reach + length],
            (((0,), (0,)), ((), ())),
            preferred_element_type=jnp.float32,
        )
    return total


def weight_taps(padded, grad_bf, reach, length):
    blocks = []
    for tap in range(3):
        blocks.append(
            lax.dot_general(
                grad_bf,
                padded[:, tap * reach : tap * reach + length],
                (((1,), (1,)), ((), ())),
                preferred_element_type=jnp.float32,
            )
        )
    return jnp.stack(blocks, axis=1)


def local(
    sequence_in,
    conv_weight,
    norm_gain,
    tissue_scale,
    donor_offset,
    acceptor_owner,
    acceptor_offset,
    tissue,
    tower_grad,
    score_grad,
):
    local_ch = sequence_in.shape[0]
    length = sequence_in.shape[1]
    seq_count = lax.axis_size("seq")
    state = sequence_in
    stored = []
    for layer in range(LAYERS):
        reach = 2 ** (layer + 3)
        stream = state.astype(jnp.float32)
        power = lax.psum(jnp.sum(stream * stream, axis=0), "tp") / CHANNELS
        inverse = 1.0 / jnp.sqrt(power + EPSILON)
        pre_act = stream * inverse[None, :] * norm_gain[layer][:, None]
        hidden = gelu_fn(pre_act).astype(jnp.bfloat16)
        padded = widen(hidden, reach)
        weights = conv_weight[layer]
        gathered = padded

        def fold_inputs(total, piece, start, weights=weights, reach=reach):
            return forward_taps(weights, piece, reach, length)

        mixed = fold_inputs(
            jnp.zeros((local_ch, length), jnp.float32),
            lax.all_gather(padded, "tp", axis=0, tiled=True),
            jnp.int32(0),
        )
        stored.append((state, inverse, pre_act, gathered))
        state = (stream + mixed).astype(jnp.bfloat16)
    owner = acceptor_owner[:, 0]
    member = (owner[:, None] == jnp.arange(seq_count, dtype=jnp.int32)[None, :]).astype(jnp.int32)
    slot = jnp.sum(jnp.cumsum(member, axis=0) * member, axis=1) - 1
    requests = jnp.zeros((seq_count, CAP), jnp.int32).at[owner, slot].set(acceptor_offset)
    rows_view = state.T
    offsets = lax.all_to_all(requests, "seq", split_axis=0, concat_axis=0, tiled=True)
    picked = rows_view[offsets]
    returned = lax.all_to_all(picked, "seq", split_axis=0, concat_axis=0, tiled=True)
    accept_cols = returned[owner, slot].astype(jnp.float32)
    donor_cols = rows_view[donor_offset].astype(jnp.float32)
    chan_start = lax.axis_index("tp") * local_ch
    local_table = lax.dynamic_slice_in_dim(tissue_scale, chan_start, local_ch, 1)
    tissue_hit = (
        tissue[:, None] == jnp.arange(tissue_scale.shape[0], dtype=jnp.int32)[None, :]
    ).astype(jnp.float32)
    tissue_rows = jnp.dot(tissue_hit, local_table, precision=lax.Precision.HIGHEST)
    root = math.sqrt(CHANNELS)
    partial_scores = jnp.sum(donor_cols * accept_cols * tissue_rows, axis=1) / root
    scores = lax.psum(partial_scores, "tp")
    weight_j = score_grad / root
    donor_back = weight_j[:, None] * accept_cols * tissue_rows
    accept_back = weight_j[:, None] * donor_cols * tissue_rows
    outgoing = jnp.zeros((seq_count, CAP, local_ch), jnp.float32).at[owner, slot].set(accept_back)
    incoming = lax.all_to_all(
        outgoing.astype(jnp.bfloat16), "seq", split_axis=0, concat_axis=0, tiled=True
    ).astype(outgoing.dtype)
    upstream = tower_grad.at[:, donor_offset].add(donor_back.T)
    upstream = upstream.at[:, offsets.reshape(-1)].add(incoming.reshape(-1, local_ch).T)
    weight_list = [None] * LAYERS
    gain_list = [None] * LAYERS
    for layer in reversed(range(LAYERS)):
        reach = 2 ** (layer + 3)
        old_state, inverse, pre_act, gathered = stored[layer]
        stream = old_state.astype(jnp.float32)
        grad_bf = upstream.astype(jnp.bfloat16)
        grad_pad = widen(grad_bf, reach)
        weights = conv_weight[layer]

        def term_rows(start, count, weights=weights, grad_pad=grad_pad, reach=reach):
            return backward_taps(weights, grad_pad, reach, length)

        back_hidden = lax.psum_scatter(
            term_rows(jnp.int32(0), local_ch * lax.axis_size("tp")).astype(jnp.bfloat16),
            "tp",
            scatter_dimension=0,
            tiled=True,
        ).astype(jnp.float32)

        def fold_weights(total, piece, start, grad_bf=grad_bf, reach=reach):
            return weight_taps(piece, grad_bf, reach, length)

        weight_term = fold_weights(
            jnp.zeros((local_ch, 3, CHANNELS), jnp.float32),
            lax.all_gather(gathered, "tp", axis=0, tiled=True),
            jnp.int32(0),
        )
        weight_list[layer] = lax.psum(weight_term.astype(jnp.bfloat16), "seq").astype(jnp.float32)
        _, gelu_back = jax.vjp(gelu_fn, pre_act)
        back_pre = gelu_back(back_hidden)[0]
        gain_list[layer] = jnp.sum(back_pre * stream * inverse[None, :], axis=1)
        back_norm = back_pre * norm_gain[layer][:, None]
        inner = lax.psum(jnp.sum(back_norm * stream, axis=0), "tp")
        upstream = (
            upstream
            + inverse[None, :] * back_norm
            - stream * (inverse**3)[None, :] * inner[None, :] / CHANNELS
        )
    gain_grad = lax.psum(jnp.stack(gain_list), "seq")
    return (scores, upstream, jnp.stack(weight_list), gain_grad)


def solution(mesh):
    return jax.shard_map(
        local,
        mesh=mesh,
        in_specs=(
            P("tp", "seq"),
            P(None, "tp", None, None),
            P(None, "tp"),
            P(),
            P("seq"),
            P("seq", None),
            P("seq"),
            P("seq"),
            P("tp", "seq"),
            P("seq"),
        ),
        out_specs=(P("seq"), P("tp", "seq"), P(None, "tp", None, None), P(None, "tp")),
        check_vma=False,
    )
```

profile of v0, /device:TPU:0, one launch (start us, length us, event | category | flops | bytes accessed | tf_op | source)
XLA Modules:
  0.0 813.4 jit_solution(14602728577334916671)
XLA Ops:
  9.6 40.8 %psum.77 = f32[512]{0:T(512)S(1)} all-reduce(f32[512]{0:T(512)S(1)} %fusion.133), channel_id=1, replica_groups=mesh['seq'=8,'tp'=16] {'tp'}, use_global_device_ids=true, to_apply=%region_1.0 | all-reduce | flops 512 | bytes 4096 | tf_op jit(solution)/shard_map/psum | solution.py:91
  54.7 3.9 collective-permute-done.1
  59.5 3.2 slice_bitcast_fusion
  62.6 40.5 %all-gather.4.cloned.1.call-done = bf16[1536,528]{1,0:T(8,128)(2,1)} async-done(((bf16[96,528]{1,0:T(8,128)(2,1)}), bf16[1536,528]{1,0:T(8,128)(2,1)}) %all-gather.4.cloned.1.call-update) | async-done | bytes 1622032 | tf_op jit(solution)/shard_map/all_gather | solution.py:104
  103.1 2.4 fusion.37
  105.6 2.2 fusion.40
  108.2 38.1 %psum.78 = f32[512]{0:T(512)S(1)} all-reduce(f32[512]{0:T(512)S(1)} %get-tuple-element.50), channel_id=1, replica_groups=mesh['seq'=8,'tp'=16] {'tp'}, use_global_device_ids=true, to_apply=%region_3.0 | all-reduce | flops 512 | bytes 4096 | tf_op jit(solution)/shard_map/psum | solution.py:91
  149.7 3.6 collective-permute-done.3
  154.1 42.9 %all-gather.6.cloned.1.call-done = bf16[1536,544]{1,0:T(8,128)(2,1)} async-done(((bf16[96,544]{1,0:T(8,128)(2,1)}), bf16[1536,544]{1,0:T(8,128)(2,1)}) %all-gather.6.cloned.1.call-update) | async-done | bytes 1671184 | tf_op jit(solution)/shard_map/all_gather | solution.py:104
  197.1 2.3 fusion.28
  200.5 38.3 %psum.79 = f32[512]{0:T(512)S(1)} all-reduce(f32[512]{0:T(512)S(1)} %get-tuple-element.52), channel_id=1, replica_groups=mesh['seq'=8,'tp'=16] {'tp'}, use_global_device_ids=true, to_apply=%region_5.0 | all-reduce | flops 512 | bytes 4096 | tf_op jit(solution)/shard_map/psum | solution.py:91
  242.9 3.6 collective-permute-done.5
  248.8 38.6 %scatter_fusion = s32[8,128]{1,0:T(8,128)} fusion(s32[8,128]{1,0:T(8,128)} %broadcast.150, s32[256]{0:T(256)S(1)} %bitcast.150, s32[256]{0:T(256)} %param.16), kind=kCustom, calls=%fused_computation.3 | custom fusion | bytes 5120 | tf_op jit(solution)/shard_map/scatter | solution.py:112
  287.5 6.3 all-to-all-start
  294.4 4.6 all-to-all-done
  299.1 2.4 fusion.19
  301.5 2.2 fusion.22
  304.2 3.2 gather_fusion.1
  308.3 3.4 all-to-all-start.1
  312.7 5.7 all-to-all-done.1
  318.6 1.7 gather_fusion.2
  322.2 16.8 %scatter_fusion.2 = f32[8,128,96]{2,1,0:T(8,128)S(1)} fusion(f32[8,128,96]{2,1,0:T(8,128)S(1)} %broadcast_in_dim.5, s32[256]{0:T(256)S(1)} %bitcast.151, f32[256,96]{1,0:T(8,128)} %copy.100), kind=kCustom, calls=%fused_computation.5 | custom fusion | bytes 296960 | tf_op jit(solution)/shard_map/scatter | solution.py:131
  339.8 4.0 all-to-all-start.2
  344.0 2.4 scatter_fusion.1
  346.4 4.3 all-to-all-done.2
  351.7 6.3 scatter_fusion.3
  358.1 2.7 collective-permute-start.7
  360.8 1.6 fusion.104
  364.3 1.7 collective-permute-done.6
  366.0 1.8 fusion.6
  368.0 71.8 %reduce-scatter.4.cloned.1.call-done = bf16[96,512]{1,0:T(8,128)(2,1)} async-done(((bf16[1536,512]{1,0:T(8,128)(2,1)}), bf16[96,512]{1,0:T(8,128)(2,1)}) %reduce-scatter.4.cloned.1.call-update) | async-done | bytes 98320 | tf_op jit(solution)/shard_map/reduce_scatter | solution.py:150
  441.0 38.1 %psum.81 = f32[512]{0:T(512)S(1)} all-reduce(f32[512]{0:T(512)S(1)} %get-tuple-element.7), channel_id=1, replica_groups=mesh['seq'=8,'tp'=16] {'tp'}, use_global_device_ids=true, to_apply=%region_17.18 | all-reduce | flops 512 | bytes 4096 | tf_op jit(solution)/shard_map/psum | solution.py:170
  479.2 1.8 fusion.168
  482.5 1.6 fusion.102
  486.1 2.9 collective-permute-done.8
  488.9 1.8 fusion.7
  490.9 2.6 fusion.16
  499.2 64.4 %reduce-scatter.6.cloned.1.call-done = bf16[96,512]{1,0:T(8,128)(2,1)} async-done(((bf16[1536,512]{1,0:T(8,128)(2,1)}), bf16[96,512]{1,0:T(8,128)(2,1)}) %reduce-scatter.6.cloned.1.call-update) | async-done | bytes 98320 | tf_op jit(solution)/shard_map/reduce_scatter | solution.py:150
  564.9 38.3 %psum.82 = f32[512]{0:T(512)S(1)} all-reduce(f32[512]{0:T(512)S(1)} %get-tuple-element.5), channel_id=1, replica_groups=mesh['seq'=8,'tp'=16] {'tp'}, use_global_device_ids=true, to_apply=%region_20.21 | all-reduce | flops 512 | bytes 4096 | tf_op jit(solution)/shard_map/psum | solution.py:170
  604.6 2.3 fusion.10
  613.4 2.9 collective-permute-done.10
  616.3 1.8 fusion.8
  618.1 55.7 %all-reduce.4.cloned.1.call-done = (bf16[1,96,3,1536]{3,1,2,0:T(8,128)(2,1)}, bf16[1,96,3,1536]{3,1,2,0:T(8,128)(2,1)}, bf16[1,96,3,1536]{3,1,2,0:T(8,128)(2,1)}) async-done(((bf16[1,96,3,1536]{3,1,2,0:T(8,128)(2,1)}, bf16[1,96,3,1536]{3,1,2,0:T(8,128)(2,1)}, bf16[1,96,3,1536]{3,1,2,0:T(8,128)(2,1)}), (bf16[1,96,3,1536]{3,1,2,0:T(8,128)(2,1)}, bf16[1,96,3,1536]{3,1,2,0:T(8,128)(2,1)}, ...) | async-done | bytes 2654224 | tf_op jit(solution)/shard_map/psum | solution.py:165
  673.8 4.5 maximum_convert_fusion
  678.3 72.7 %reduce-scatter.8.cloned.1.call-done = bf16[96,512]{1,0:T(8,128)(2,1)} async-done(((bf16[1536,512]{1,0:T(8,128)(2,1)}), bf16[96,512]{1,0:T(8,128)(2,1)}) %reduce-scatter.8.cloned.1.call-update) | async-done | bytes 98320 | tf_op jit(solution)/shard_map/reduce_scatter | solution.py:150
  752.3 13.7 %psum.87 = f32[3,96]{1,0:T(4,128)} all-reduce(f32[3,96]{1,0:T(4,128)S(1)} %pad_maximum_fusion.15), channel_id=1, replica_groups=mesh['seq'=8,'tp'=16] {'seq'}, use_global_device_ids=true, to_apply=%region_30.31 | all-reduce | flops 288 | bytes 2304 | tf_op jit(solution)/shard_map/psum | solution.py:176
  766.1 38.6 %all-reduce = (f32[256]{0:T(256)}, f32[512]{0:T(512)S(1)}) all-reduce(f32[256]{0:T(256)S(1)} %broadcast_multiply_fusion.1, f32[512]{0:T(512)S(1)} %get-tuple-element.9), channel_id=1, replica_groups=mesh['seq'=8,'tp'=16] {'tp'}, use_global_device_ids=true, to_apply=%region_11.12 | all-reduce | flops 768 | bytes 6144 | tf_op jit(solution)/shard_map/psum | solution.py:127
  804.7 1.8 fusion.139
  (168 shorter events, 49.5 us)
Async XLA Ops:
  7.2 313.2 %copy-start = (f32[367,1536]{1,0:T(8,128)S(1)}, f32[367,1536]{1,0:T(8,128)}, u32[]{:S(2)}) copy-start(f32[367,1536]{1,0:T(8,128)} %param.13) | copy-start | bytes 6764548
  7.2 96.0 %all-gather.4.cloned.1.call-start = ((), (), s32[]{:S(2)}) async-start(), calls=%async_computation.6 | async-start | bytes 2088960 | tf_op jit(solution)/shard_map/all_gather | solution.py:104
  8.7 54.0 %copy-start.22 = (f32[96]{0:T(128)}, f32[96]{0:T(128)S(1)}, u32[]{:S(2)}) copy-start(f32[96]{0:T(128)S(1)} %get-tuple-element.46) | copy-start | bytes 1156
  8.7 138.3 %copy-start.24 = (f32[96]{0:T(128)}, f32[96]{0:T(128)S(1)}, u32[]{:S(2)}) copy-start(f32[96]{0:T(128)S(1)} %get-tuple-element.47) | copy-start | bytes 1156
  52.1 2.6 collective-permute-start
  53.4 5.2 collective-permute-start.1
  59.4 137.7 %all-gather.6.cloned.1.call-start = ((), (), s32[]{:S(2)}) async-start(), calls=%async_computation.7 | async-start | bytes 2088960 | tf_op jit(solution)/shard_map/all_gather | solution.py:104
  62.6 137.5 %copy-start.1 = (bf16[96,3,1536]{2,0,1:T(8,128)(2,1)}, bf16[96,3,1536]{2,0,1:T(8,128)(2,1)S(1)}, u32[]{:S(2)}) copy-start(bf16[96,3,1536]{2,0,1:T(8,128)(2,1)S(1)} %get-tuple-element.23) | copy-start | bytes 2654212
  103.1 4.6 copy-start.7
  103.1 4.6 copy-start.31
  147.1 2.6 collective-permute-start.2
  148.4 4.9 collective-permute-start.3
  154.1 145.0 %all-gather.8.cloned.1.call-start = ((), (), s32[]{:S(2)}) async-start(), calls=%async_computation.8 | async-start | bytes 2088960 | tf_op jit(solution)/shard_map/all_gather | solution.py:104
  200.1 47.2 %copy-start.18 = (s32[256,1]{0,1:T(1,128)S(1)}, s32[256,1]{0,1:T(1,128)}, u32[]{:S(2)}) copy-start(s32[256,1]{0,1:T(1,128)} %param.15) | copy-start | bytes 3076
  200.5 93.3 %copy-start.29 = (s32[256]{0:T(256)S(1)}, s32[256]{0:T(256)}, u32[]{:S(2)}) copy-start(s32[256]{0:T(256)} %param.14) | copy-start | bytes 3076
  200.5 93.8 %copy-start.14 = (f32[96,512]{1,0:T(8,128)S(1)}, f32[96,512]{1,0:T(8,128)}, u32[]{:S(2)}) copy-start(f32[96,512]{1,0:T(8,128)} %param.18) | copy-start | bytes 589828
  239.4 7.8 copy-start.15
  240.3 2.6 collective-permute-start.4
  241.6 4.9 collective-permute-start.5
  287.5 11.6 %all-to-all-start = ((s32[8,1,128]{2,1,0:T(1,128)}), s32[8,1,128]{2,1,0:T(1,128)S(1)}, u32[]{:S(2)}, u32[]{:S(2)}) async-start(s32[8,1,128]{2,1,0:T(1,128)} %bitcast.27), calls=%async_computation | async-start | bytes 8192 | tf_op jit(solution)/shard_map/all_to_all | solution.py:114
  299.1 4.6 copy-start.11
  304.1 7.6 copy-start.30
  307.5 12.9 %copy-start.28 = (s32[256]{0:T(256)S(1)}, s32[256]{0:T(256)}, u32[]{:S(2)}) copy-start(s32[256]{0:T(256)} %param.17) | copy-start | bytes 3076
  308.3 10.1 %all-to-all-start.1 = ((bf16[8,128,96]{1,2,0:T(8,128)(2,1)}), bf16[8,128,96]{1,2,0:T(8,128)(2,1)S(1)}, u32[]{:S(2)}, u32[]{:S(2)}) async-start(bf16[8,128,96]{1,2,0:T(8,128)(2,1)} %copy.95), calls=%async_computation.1 | async-start | bytes 393216 | tf_op jit(solution)/shard_map/all_to_all | solution.py:116
  339.8 10.8 %all-to-all-start.2 = ((bf16[8,128,96]{1,2,0:T(8,128)(2,1)}), bf16[8,128,96]{1,2,0:T(8,128)(2,1)}, u32[]{:S(2)}, u32[]{:S(2)}) async-start(bf16[8,128,96]{1,2,0:T(8,128)(2,1)} %copy.101), calls=%async_computation.2 | async-start | bytes 393216 | tf_op jit(solution)/shard_map/all_to_all | solution.py:132
  343.9 95.9 %reduce-scatter.4.cloned.1.call-start = ((), (), s32[]{:S(2)}) async-start(), calls=%async_computation.9 | async-start | bytes 1671168 | tf_op jit(solution)/shard_map/reduce_scatter | solution.py:150
  358.1 5.6 copy-start.4
  358.1 5.6 collective-permute-start.7
  362.4 3.6 collective-permute-start.6
  367.8 72.0 %copy-start.16 = (f32[512]{0:T(512)S(1)}, f32[512]{0:T(512)}, u32[]{:S(2)}) copy-start(f32[512]{0:T(512)} %copy-done.15) | copy-start | bytes 6148
  367.8 72.0 %copy-start.26 = (f32[96]{0:T(128)S(1)}, f32[96]{0:T(128)}, u32[]{:S(2)}) copy-start(f32[96]{0:T(128)} %get-tuple-element.45) | copy-start | bytes 1156
  367.8 111.4 %copy-start.21 = (f32[512]{0:T(512)S(1)}, f32[512]{0:T(512)}, u32[]{:S(2)}) copy-start(f32[512]{0:T(512)} %get-tuple-element.43) | copy-start | bytes 6148
  367.8 195.9 %reduce-scatter.6.cloned.1.call-start = ((), (), s32[]{:S(2)}) async-start(), calls=%async_computation.10 | async-start | bytes 1671168 | tf_op jit(solution)/shard_map/reduce_scatter | solution.py:150
  481.0 4.4 copy-start.2
  481.1 4.3 collective-permute-start.9
  484.1 4.9 collective-permute-start.8
  490.8 183.0 %all-reduce.4.cloned.1.call-start = ((), (), s32[]{:S(2)}) async-start(), calls=%async_computation.12 | async-start | bytes 5308416 | tf_op jit(solution)/shard_map/psum | solution.py:165
  497.4 66.3 %copy-start.25 = (f32[96]{0:T(128)S(1)}, f32[96]{0:T(128)}, u32[]{:S(2)}) copy-start(f32[96]{0:T(128)} %copy-done.24) | copy-start | bytes 1156
  497.4 105.9 %copy-start.13 = (f32[96,512]{1,0:T(8,128)S(1)}, f32[96,512]{1,0:T(8,128)}, u32[]{:S(2)}) copy-start(f32[96,512]{1,0:T(8,128)} %get-tuple-element.18) | copy-start | bytes 589828
  497.4 105.9 %copy-start.20 = (f32[512]{0:T(512)S(1)}, f32[512]{0:T(512)}, u32[]{:S(2)}) copy-start(f32[512]{0:T(512)} %get-tuple-element.41) | copy-start | bytes 6148
  603.3 3.6 copy-start.32
  609.3 141.7 %reduce-scatter.8.cloned.1.call-start = ((), (), s32[]{:S(2)}) async-start(), calls=%async_computation.11 | async-start | bytes 1671168 | tf_op jit(solution)/shard_map/reduce_scatter | solution.py:150
  609.5 3.2 collective-permute-start.11
  611.4 4.9 collective-permute-start.10
  613.4 4.8 copy-start.27
  673.8 77.3 %copy-start.8 = (bf16[96,512]{1,0:T(8,128)(2,1)S(1)}, bf16[96,512]{1,0:T(8,128)(2,1)}, u32[]{:S(2)}) copy-start(bf16[96,512]{1,0:T(8,128)(2,1)} %param.10) | copy-start | bytes 294916
  673.8 77.3 %copy-start.23 = (f32[96]{0:T(128)S(1)}, f32[96]{0:T(128)}, u32[]{:S(2)}) copy-start(f32[96]{0:T(128)} %copy-done.22) | copy-start | bytes 1156
  673.8 130.9 %copy-start.19 = (f32[512]{0:T(512)S(1)}, f32[512]{0:T(512)}, u32[]{:S(2)}) copy-start(f32[512]{0:T(512)} %get-tuple-element.39) | copy-start | bytes 6148
  (7 other events, 14.7 us)
Sparse Core Ops, SparseCore 0:
  59.5 43.5 all-gather.3
  154.2 42.8 all-gather.5
  247.4 42.8 all-gather.7
  367.9 71.7 reduce-scatter.3
  490.9 72.7 reduce-scatter.5
  609.5 64.2 all-reduce.3
  677.0 73.9 reduce-scatter.7
where the time goes:
time: 816 us; the launch traced here: 813 us
  waiting for transfers between devices  381 us (47%)
  blocking collectives  246 us (30%)
  local copies, waits for them, and re-layouts  71.9 us (9%)
  matrix products  35.4 us (4%)
  other arithmetic  32.8 us (4%)
  starting transfers between devices  30.9 us (4%)
  between operations  14.9 us (2%)
    reduce_scatter x3, waiting for transfers between devices, local(): lax.psum_scatter(term_rows(jnp.int32(0), local_ch * lax.axis_size('tp'))....  209 us
    psum x3, blocking collectives, local(): power = lax.psum(jnp.sum(stream * stream, axis=0), 'tp') / CHANNELS  117 us
    all_gather x3, waiting for transfers between devices, local(): lax.all_gather(padded, 'tp', axis=0, tiled=True)  83.4 us
    psum x2, blocking collectives, local(): inner = lax.psum(jnp.sum(back_norm * stream, axis=0), 'tp')  76.5 us
    psum x1, waiting for transfers between devices, local(): lax.psum(weight_term.astype(jnp.bfloat16), 'seq').astype(jnp.float32)  55.7 us
    psum x1, blocking collectives, local(): scores = lax.psum(partial_scores, 'tp')  38.6 us
    scatter x1, local copies, waits for them, and re-layouts, local(): jnp.zeros((seq_count, CAP), jnp.int32).at[owner, slot].set(acceptor_offset)  38.6 us
    ppermute x6, waiting for transfers between devices, with_halo(): after = lax.ppermute(initial, axis, down)  18.6 us
  transfers between devices with their start and end apart: 22, of which 15 were waited for; matrix products, arithmetic and copies ran while one was open for 8% of the time, Pallas kernels for 0%

commit v1 on v0

--- a/solution.py
+++ b/solution.py
@@ -8,6 +8,13 @@
 LAYERS = 3
 CAP = 128
 EPSILON = 1e-06
+
+
+def swapped_in(x, axis, dim):
+    size = lax.axis_size(axis)
+    parts = jnp.stack([x for _ in range(size)])
+    parts = lax.all_to_all(parts, axis, split_axis=0, concat_axis=0)
+    return jnp.concatenate(parts, axis=dim)
 
 
 def with_halo(x, sides, width):
@@ -100,9 +107,7 @@
             return forward_taps(weights, piece, reach, length)
 
         mixed = fold_inputs(
-            jnp.zeros((local_ch, length), jnp.float32),
-            lax.all_gather(padded, "tp", axis=0, tiled=True),
-            jnp.int32(0),
+            jnp.zeros((local_ch, length), jnp.float32), swapped_in(padded, "tp", 0), jnp.int32(0)
         )
         stored.append((state, inverse, pre_act, gathered))
         state = (stream + mixed).astype(jnp.bfloat16)

time: 816 us -> 888 us (1.088)
  waiting for transfers between devices: 381 us -> 420 us
  starting transfers between devices: 30.9 us -> 48.7 us
    all_to_all x0 -> x3, waiting for transfers between devices: none -> 80.4 us  [swapped_in(): parts = lax.all_to_all(parts, axis, split_axis=0, concat_axis=0)]
    all_gather x3, waiting for transfers between devices: 83.4 us -> 42.3 us  [local(): lax.all_gather(gathered, 'tp', axis=0, tiled=True)]
    all_to_all x0 -> x3, starting transfers between devices: none -> 13.5 us  [swapped_in(): parts = lax.all_to_all(parts, axis, split_axis=0, concat_axis=0)]
    ppermute x6, waiting for transfers between devices: 18.6 us -> 7.51 us  [with_halo(): after = lax.ppermute(initial, axis, down)]
  transfers between devices with their start and end apart: 22 -> 25, of which waited for: 15 -> 17; matrix products, arithmetic and copies ran while one was open for 8% -> 9% of each run, Pallas kernels for 0% -> 0%
where the time goes in v1:
time: 888 us; the launch traced here: 885 us
  waiting for transfers between devices  420 us (47%)
  blocking collectives  244 us (27%)
  local copies, waits for them, and re-layouts  80.6 us (9%)
  starting transfers between devices  48.7 us (5%)
  matrix products  42.4 us (5%)
  other arithmetic  34.2 us (4%)
  between operations  14.9 us (2%)
    reduce_scatter x3, waiting for transfers between devices, local(): lax.psum_scatter(term_rows(jnp.int32(0), local_ch * lax.axis_size('tp'))....  217 us
    psum x3, blocking collectives, local(): power = lax.psum(jnp.sum(stream * stream, axis=0), 'tp') / CHANNELS  115 us
    all_to_all x3, waiting for transfers between devices, swapped_in(): parts = lax.all_to_all(parts, axis, split_axis=0, concat_axis=0)  80.4 us
    psum x2, blocking collectives, local(): inner = lax.psum(jnp.sum(back_norm * stream, axis=0), 'tp')  76.4 us
    psum x1, waiting for transfers between devices, local(): lax.psum(weight_term.astype(jnp.bfloat16), 'seq').astype(jnp.float32)  58.8 us
    all_gather x3, waiting for transfers between devices, local(): lax.all_gather(gathered, 'tp', axis=0, tiled=True)  42.3 us
    scatter x1, local copies, waits for them, and re-layouts, local(): jnp.zeros((seq_count, CAP), jnp.int32).at[owner, slot].set(acceptor_offset)  38.7 us
    psum x1, blocking collectives, local(): scores = lax.psum(partial_scores, 'tp')  38.6 us
  transfers between devices with their start and end apart: 25, of which 17 were waited for; matrix products, arithmetic and copies ran while one was open for 9% of the time, Pallas kernels for 0%

profile of v1, /device:TPU:0, one launch (start us, length us, event | category | flops | bytes accessed | tf_op | source)
XLA Modules:
  0.0 884.7 jit_solution(8979634329239232484)
XLA Ops:
  9.5 40.8 %psum.77 = f32[512]{0:T(512)S(1)} all-reduce(f32[512]{0:T(512)S(1)} %fusion.133), channel_id=1, replica_groups=mesh['seq'=8,'tp'=16] {'tp'}, use_global_device_ids=true, to_apply=%region_1.0 | all-reduce | flops 512 | bytes 4096 | tf_op jit(solution)/shard_map/psum | solution.py:98
  53.3 3.0 collective-permute-start
  58.7 4.4 all-to-all-start
  63.1 3.1 slice_bitcast_fusion
  66.2 25.8 %all-to-all-done = bf16[16,96,528]{2,1,0:T(8,128)(2,1)} async-done(((bf16[16,96,528]{2,1,0:T(8,128)(2,1)}), bf16[16,96,528]{2,1,0:T(8,128)(2,1)}, u32[]{:S(2)}, u32[]{:S(2)}) %all-to-all-start) | async-done | bytes 1622048 | tf_op jit(solution)/shard_map/all_to_all | solution.py:16
  92.1 2.2 fusion.41
  96.1 2.2 multiply_reduce_fusion.5
  98.3 37.8 %psum.78 = f32[512]{0:T(512)S(1)} all-reduce(f32[512]{0:T(512)S(1)} %get-tuple-element.50), channel_id=1, replica_groups=mesh['seq'=8,'tp'=16] {'tp'}, use_global_device_ids=true, to_apply=%region_3.0 | all-reduce | flops 512 | bytes 4096 | tf_op jit(solution)/shard_map/psum | solution.py:98
  138.2 3.0 collective-permute-start.2
  143.6 4.6 all-to-all-start.1
  149.7 27.6 %all-to-all-done.1 = bf16[16,96,544]{2,1,0:T(8,128)(2,1)} async-done(((bf16[16,96,544]{2,1,0:T(8,128)(2,1)}), bf16[16,96,544]{2,1,0:T(8,128)(2,1)}, u32[]{:S(2)}, u32[]{:S(2)}) %all-to-all-start.1) | async-done | bytes 1671200 | tf_op jit(solution)/shard_map/all_to_all | solution.py:16
  177.4 2.4 fusion.35
  181.5 2.2 multiply_reduce_fusion.4
  183.8 36.3 %psum.79 = f32[512]{0:T(512)S(1)} all-reduce(f32[512]{0:T(512)S(1)} %get-tuple-element.52), channel_id=1, replica_groups=mesh['seq'=8,'tp'=16] {'tp'}, use_global_device_ids=true, to_apply=%region_5.0 | all-reduce | flops 512 | bytes 4096 | tf_op jit(solution)/shard_map/psum | solution.py:98
  222.8 3.6 collective-permute-start.4
  227.7 38.7 %scatter_fusion = s32[8,128]{1,0:T(8,128)} fusion(s32[8,128]{1,0:T(8,128)} %broadcast.156, s32[256]{0:T(256)S(1)} %bitcast.151, s32[256]{0:T(256)} %param.16), kind=kCustom, calls=%fused_computation.3 | custom fusion | bytes 5120 | tf_op jit(solution)/shard_map/scatter | solution.py:117
  266.4 4.6 all-to-all-start.3
  272.5 3.8 all-to-all-done.3
  277.7 4.6 all-to-all-start.2
  284.5 27.0 %all-to-all-done.2 = bf16[16,96,576]{2,1,0:T(8,128)(2,1)} async-done(((bf16[16,96,576]{2,1,0:T(8,128)(2,1)}), bf16[16,96,576]{2,1,0:T(8,128)(2,1)}, u32[]{:S(2)}, u32[]{:S(2)}) %all-to-all-start.2) | async-done | bytes 1769504 | tf_op jit(solution)/shard_map/all_to_all | solution.py:16
  311.5 2.4 fusion.29
  315.7 2.8 fusion.96
  319.6 4.6 gather_fusion.1
  326.0 4.2 all-to-all-start.4
  334.6 2.2 all-to-all-done.4
  338.6 2.6 gather_fusion.2
  344.9 12.3 %scatter_fusion.2 = f32[8,128,96]{2,1,0:T(8,128)S(1)} fusion(f32[8,128,96]{2,1,0:T(8,128)S(1)} %broadcast_in_dim.5, s32[256]{0:T(256)S(1)} %bitcast.152, f32[256,96]{1,0:T(8,128)S(1)} %copy.100), kind=kCustom, calls=%fused_computation.5 | custom fusion | bytes 296960 | tf_op jit(solution)/shard_map/scatter | solution.py:136
  358.0 3.4 all-to-all-start.5
  361.6 2.0 scatter_fusion.1
  363.7 4.5 all-to-all-done.5
  368.3 6.3 scatter_fusion.3
  374.7 2.5 collective-permute-start.7
  385.0 71.8 %reduce-scatter.4.cloned.1.call-done = bf16[96,512]{1,0:T(8,128)(2,1)} async-done(((bf16[1536,512]{1,0:T(8,128)(2,1)}), bf16[96,512]{1,0:T(8,128)(2,1)}) %reduce-scatter.4.cloned.1.call-update) | async-done | bytes 98320 | tf_op jit(solution)/shard_map/reduce_scatter | solution.py:155
  458.0 38.2 %psum.81 = f32[512]{0:T(512)S(1)} all-reduce(f32[512]{0:T(512)S(1)} %get-tuple-element.7), channel_id=1, replica_groups=mesh['seq'=8,'tp'=16] {'tp'}, use_global_device_ids=true, to_apply=%region_17.18 | all-reduce | flops 512 | bytes 4096 | tf_op jit(solution)/shard_map/psum | solution.py:175
  501.4 2.9 collective-permute-done.8
  507.0 2.6 fusion.17
  512.2 36.9 %all-gather.6.cloned.1.call-done = bf16[1536,544]{1,0:T(8,128)(2,1)} async-done(((bf16[96,544]{1,0:T(8,128)(2,1)}), bf16[1536,544]{1,0:T(8,128)(2,1)}) %all-gather.6.cloned.1.call-update) | async-done | bytes 1671184 | tf_op jit(solution)/shard_map/all_gather | solution.py:167
  549.1 2.5 fusion.14
  554.0 72.6 %reduce-scatter.6.cloned.1.call-done = bf16[96,512]{1,0:T(8,128)(2,1)} async-done(((bf16[1536,512]{1,0:T(8,128)(2,1)}), bf16[96,512]{1,0:T(8,128)(2,1)}) %reduce-scatter.6.cloned.1.call-update) | async-done | bytes 98320 | tf_op jit(solution)/shard_map/reduce_scatter | solution.py:155
  627.9 38.2 %psum.82 = f32[512]{0:T(512)S(1)} all-reduce(f32[512]{0:T(512)S(1)} %get-tuple-element.5), channel_id=1, replica_groups=mesh['seq'=8,'tp'=16] {'tp'}, use_global_device_ids=true, to_apply=%region_20.21 | all-reduce | flops 512 | bytes 4096 | tf_op jit(solution)/shard_map/psum | solution.py:175
  667.3 5.4 all-gather.4.cloned.1.call-done
  672.7 2.5 fusion.11
  681.6 2.9 collective-permute-done.10
  686.3 58.8 %all-reduce.4.cloned.1.call-done = (bf16[1,96,3,1536]{3,1,2,0:T(8,128)(2,1)}, bf16[1,96,3,1536]{3,1,2,0:T(8,128)(2,1)}, bf16[1,96,3,1536]{3,1,2,0:T(8,128)(2,1)}) async-done(((bf16[1,96,3,1536]{3,1,2,0:T(8,128)(2,1)}, bf16[1,96,3,1536]{3,1,2,0:T(8,128)(2,1)}, bf16[1,96,3,1536]{3,1,2,0:T(8,128)(2,1)}), (bf16[1,96,3,1536]{3,1,2,0:T(8,128)(2,1)}, bf16[1,96,3,1536]{3,1,2,0:T(8,128)(2,1)}, ...) | async-done | bytes 2654224 | tf_op jit(solution)/shard_map/psum | solution.py:170
  745.1 4.6 maximum_convert_fusion
  749.8 72.6 %reduce-scatter.8.cloned.1.call-done = bf16[96,512]{1,0:T(8,128)(2,1)} async-done(((bf16[1536,512]{1,0:T(8,128)(2,1)}), bf16[96,512]{1,0:T(8,128)(2,1)}) %reduce-scatter.8.cloned.1.call-update) | async-done | bytes 98320 | tf_op jit(solution)/shard_map/reduce_scatter | solution.py:155
  823.7 13.7 %psum.87 = f32[3,96]{1,0:T(4,128)} all-reduce(f32[3,96]{1,0:T(4,128)S(1)} %pad_maximum_fusion.15), channel_id=1, replica_groups=mesh['seq'=8,'tp'=16] {'seq'}, use_global_device_ids=true, to_apply=%region_30.31 | all-reduce | flops 288 | bytes 2304 | tf_op jit(solution)/shard_map/psum | solution.py:181
  837.4 38.6 %all-reduce = (f32[256]{0:T(256)}, f32[512]{0:T(512)S(1)}) all-reduce(f32[256]{0:T(256)S(1)} %broadcast_multiply_fusion.1, f32[512]{0:T(512)S(1)} %get-tuple-element.9), channel_id=1, replica_groups=mesh['seq'=8,'tp'=16] {'tp'}, use_global_device_ids=true, to_apply=%region_11.12 | all-reduce | flops 768 | bytes 6144 | tf_op jit(solution)/shard_map/psum | solution.py:132
  (187 shorter events, 77.4 us)
Async XLA Ops:
  7.2 334.7 %copy-start = (f32[367,1536]{1,0:T(8,128)S(1)}, f32[367,1536]{1,0:T(8,128)}, u32[]{:S(2)}) copy-start(f32[367,1536]{1,0:T(8,128)} %param.13) | copy-start | bytes 6764548
  8.6 42.3 %copy-start.29 = (f32[96]{0:T(128)}, f32[96]{0:T(128)S(1)}, u32[]{:S(2)}) copy-start(f32[96]{0:T(128)S(1)} %get-tuple-element.46) | copy-start | bytes 1156
  8.6 128.1 %copy-start.31 = (f32[96]{0:T(128)}, f32[96]{0:T(128)S(1)}, u32[]{:S(2)}) copy-start(f32[96]{0:T(128)S(1)} %get-tuple-element.47) | copy-start | bytes 1156
  52.0 4.3 collective-permute-start.1
  53.3 3.9 collective-permute-start
  58.7 33.4 %all-to-all-start = ((bf16[16,96,528]{2,1,0:T(8,128)(2,1)}), bf16[16,96,528]{2,1,0:T(8,128)(2,1)}, u32[]{:S(2)}, u32[]{:S(2)}) async-start(bf16[16,96,528]{2,1,0:T(8,128)(2,1)} %stack.64), calls=%async_computation | async-start | bytes 3932160 | tf_op jit(solution)/shard_map/all_to_all | solution.py:16
  98.3 83.2 %copy-start.6 = (f32[96,512]{1,0:T(8,128)}, f32[96,512]{1,0:T(8,128)S(1)}, u32[]{:S(2)}) copy-start(f32[96,512]{1,0:T(8,128)S(1)} %get-tuple-element.51) | copy-start | bytes 589828
  136.9 4.3 collective-permute-start.3
  138.2 3.9 collective-permute-start.2
  143.6 33.7 %all-to-all-start.1 = ((bf16[16,96,544]{2,1,0:T(8,128)(2,1)}), bf16[16,96,544]{2,1,0:T(8,128)(2,1)}, u32[]{:S(2)}, u32[]{:S(2)}) async-start(bf16[16,96,544]{2,1,0:T(8,128)(2,1)} %stack.65), calls=%async_computation.1 | async-start | bytes 3932160 | tf_op jit(solution)/shard_map/all_to_all | solution.py:16
  183.7 42.7 %copy-start.8 = (f32[96,512]{1,0:T(8,128)}, f32[96,512]{1,0:T(8,128)S(1)}, u32[]{:S(2)}) copy-start(f32[96,512]{1,0:T(8,128)S(1)} %get-tuple-element.53) | copy-start | bytes 589828
  220.6 57.1 %copy-start.20 = (f32[512]{0:T(512)}, f32[512]{0:T(512)S(1)}, u32[]{:S(2)}) copy-start(f32[512]{0:T(512)S(1)} %get-tuple-element.44) | copy-start | bytes 6148
  221.5 49.5 %collective-permute-start.5 = (bf16[96,32]{1,0:T(8,128)(2,1)S(1)}, bf16[96,32]{1,0:T(8,128)(2,1)S(1)}, u32[]{:S(2)}, u32[]{:S(2)}) collective-permute-start(bf16[96,32]{1,0:T(8,128)(2,1)S(1)} %get-tuple-element.34), channel_id=1, source_target_pairs={{16,0},{32,16},{48,32},{64,48},{80,64},{96,80},{112,96},{17,1},{33... | collective-permute-start | bytes 18440 | tf_op jit(solution)/shard_map/ppermute | solution.py:28
  222.8 48.8 %collective-permute-start.4 = (bf16[96,32]{1,0:T(8,128)(2,1)S(1)}, bf16[96,32]{1,0:T(8,128)(2,1)}, u32[]{:S(2)}, u32[]{:S(2)}) collective-permute-start(bf16[96,32]{1,0:T(8,128)(2,1)S(1)} %get-tuple-element.33), channel_id=1, source_target_pairs={{0,16},{16,32},{32,48},{48,64},{64,80},{80,96},{96,112},{1,17},{17... | collective-permute-start | bytes 18440 | tf_op jit(solution)/shard_map/ppermute | solution.py:27
  227.1 44.5 %copy-start.17 = (bf16[96,512]{1,0:T(8,128)(2,1)S(1)}, bf16[96,512]{1,0:T(8,128)(2,1)}, u32[]{:S(2)}) copy-start(bf16[96,512]{1,0:T(8,128)(2,1)} %copy-done.16) | copy-start | bytes 294916
  266.4 9.9 %all-to-all-start.3 = ((s32[8,1,128]{2,1,0:T(1,128)}), s32[8,1,128]{2,1,0:T(1,128)S(1)}, u32[]{:S(2)}, u32[]{:S(2)}) async-start(s32[8,1,128]{2,1,0:T(1,128)} %bitcast.30), calls=%async_computation.3 | async-start | bytes 8192 | tf_op jit(solution)/shard_map/all_to_all | solution.py:119
  277.7 33.8 %all-to-all-start.2 = ((bf16[16,96,576]{2,1,0:T(8,128)(2,1)}), bf16[16,96,576]{2,1,0:T(8,128)(2,1)}, u32[]{:S(2)}, u32[]{:S(2)}) async-start(bf16[16,96,576]{2,1,0:T(8,128)(2,1)} %stack.66), calls=%async_computation.2 | async-start | bytes 3932160 | tf_op jit(solution)/shard_map/all_to_all | solution.py:16
  283.3 32.3 %copy-start.23 = (s32[256]{0:T(256)}, s32[256]{0:T(256)S(1)}, u32[]{:S(2)}) copy-start(s32[256]{0:T(256)S(1)} %compare_select_fusion.4) | copy-start | bytes 3076
  326.0 10.8 %all-to-all-start.4 = ((bf16[8,128,96]{1,2,0:T(8,128)(2,1)}), bf16[8,128,96]{1,2,0:T(8,128)(2,1)}, u32[]{:S(2)}, u32[]{:S(2)}) async-start(bf16[8,128,96]{1,2,0:T(8,128)(2,1)} %copy.95), calls=%async_computation.4 | async-start | bytes 393216 | tf_op jit(solution)/shard_map/all_to_all | solution.py:121
  344.9 16.7 %copy-start.24 = (s32[256]{0:T(256)S(1)}, s32[256]{0:T(256)}, u32[]{:S(2)}) copy-start(s32[256]{0:T(256)} %copy-done.23) | copy-start | bytes 3076
  358.0 10.1 %all-to-all-start.5 = ((bf16[8,128,96]{1,2,0:T(8,128)(2,1)}), bf16[8,128,96]{1,2,0:T(8,128)(2,1)S(1)}, u32[]{:S(2)}, u32[]{:S(2)}) async-start(bf16[8,128,96]{1,2,0:T(8,128)(2,1)} %copy.101), calls=%async_computation.5 | async-start | bytes 393216 | tf_op jit(solution)/shard_map/all_to_all | solution.py:137
  361.4 95.3 %reduce-scatter.4.cloned.1.call-start = ((), (), s32[]{:S(2)}) async-start(), calls=%async_computation.9 | async-start | bytes 1671168 | tf_op jit(solution)/shard_map/reduce_scatter | solution.py:155
  368.3 8.9 %copy-start.5 = (bf16[96,3,1536]{2,0,1:T(8,128)(2,1)S(1)}, bf16[96,3,1536]{2,0,1:T(8,128)(2,1)}, u32[]{:S(2)}) copy-start(bf16[96,3,1536]{2,0,1:T(8,128)(2,1)} %get-tuple-element.21) | copy-start | bytes 2654212
  374.7 4.5 collective-permute-start.7
  377.9 3.6 collective-permute-start.6
  383.3 73.5 %copy-start.10 = (f32[96,512]{1,0:T(8,128)S(1)}, f32[96,512]{1,0:T(8,128)}, u32[]{:S(2)}) copy-start(f32[96,512]{1,0:T(8,128)} %copy-done.8) | copy-start | bytes 589828
  383.3 73.5 %copy-start.21 = (f32[512]{0:T(512)S(1)}, f32[512]{0:T(512)}, u32[]{:S(2)}) copy-start(f32[512]{0:T(512)} %copy-done.20) | copy-start | bytes 6148
  383.3 73.5 %copy-start.33 = (f32[96]{0:T(128)S(1)}, f32[96]{0:T(128)}, u32[]{:S(2)}) copy-start(f32[96]{0:T(128)} %get-tuple-element.45) | copy-start | bytes 1156
  383.3 113.0 %copy-start.28 = (f32[512]{0:T(512)S(1)}, f32[512]{0:T(512)}, u32[]{:S(2)}) copy-start(f32[512]{0:T(512)} %get-tuple-element.43) | copy-start | bytes 6148
  383.3 115.5 %copy-start.3 = (bf16[96,3,1536]{2,0,1:T(8,128)(2,1)S(1)}, bf16[96,3,1536]{2,0,1:T(8,128)(2,1)}, u32[]{:S(2)}) copy-start(bf16[96,3,1536]{2,0,1:T(8,128)(2,1)} %get-tuple-element.23) | copy-start | bytes 2654212
  383.3 123.7 %all-gather.8.cloned.1.call-start = ((), (), s32[]{:S(2)}) async-start(), calls=%async_computation.14 | async-start | bytes 2088960 | tf_op jit(solution)/shard_map/all_gather | solution.py:167
  384.1 165.0 %all-gather.6.cloned.1.call-start = ((), (), s32[]{:S(2)}) async-start(), calls=%async_computation.13 | async-start | bytes 2088960 | tf_op jit(solution)/shard_map/all_gather | solution.py:167
  384.8 241.8 %reduce-scatter.6.cloned.1.call-start = ((), (), s32[]{:S(2)}) async-start(), calls=%async_computation.10 | async-start | bytes 1671168 | tf_op jit(solution)/shard_map/reduce_scatter | solution.py:155
  497.5 3.2 collective-permute-start.9
  499.5 4.9 collective-permute-start.8
  506.1 166.5 %all-gather.4.cloned.1.call-start = ((), (), s32[]{:S(2)}) async-start(), calls=%async_computation.12 | async-start | bytes 2088960 | tf_op jit(solution)/shard_map/all_gather | solution.py:167
  506.7 238.4 %all-reduce.4.cloned.1.call-start = ((), (), s32[]{:S(2)}) async-start(), calls=%async_computation.15 | async-start | bytes 5308416 | tf_op jit(solution)/shard_map/psum | solution.py:170
  552.4 74.3 %copy-start.7 = (f32[96,512]{1,0:T(8,128)S(1)}, f32[96,512]{1,0:T(8,128)}, u32[]{:S(2)}) copy-start(f32[96,512]{1,0:T(8,128)} %copy-done.6) | copy-start | bytes 589828
  552.4 74.3 %copy-start.19 = (f32[512]{0:T(512)S(1)}, f32[512]{0:T(512)}, u32[]{:S(2)}) copy-start(f32[512]{0:T(512)} %copy-done.18) | copy-start | bytes 6148
  552.4 74.3 %copy-start.32 = (f32[96]{0:T(128)S(1)}, f32[96]{0:T(128)}, u32[]{:S(2)}) copy-start(f32[96]{0:T(128)} %copy-done.31) | copy-start | bytes 1156
  552.4 113.7 %copy-start.27 = (f32[512]{0:T(512)S(1)}, f32[512]{0:T(512)}, u32[]{:S(2)}) copy-start(f32[512]{0:T(512)} %get-tuple-element.41) | copy-start | bytes 6148
  677.6 144.8 %reduce-scatter.8.cloned.1.call-start = ((), (), s32[]{:S(2)}) async-start(), calls=%async_computation.11 | async-start | bytes 1671168 | tf_op jit(solution)/shard_map/reduce_scatter | solution.py:155
  677.7 3.2 collective-permute-start.11
  679.6 4.9 collective-permute-start.10
  745.1 77.3 %copy-start.12 = (bf16[96,512]{1,0:T(8,128)(2,1)S(1)}, bf16[96,512]{1,0:T(8,128)(2,1)}, u32[]{:S(2)}) copy-start(bf16[96,512]{1,0:T(8,128)(2,1)} %param.10) | copy-start | bytes 294916
  745.1 77.3 %copy-start.30 = (f32[96]{0:T(128)S(1)}, f32[96]{0:T(128)}, u32[]{:S(2)}) copy-start(f32[96]{0:T(128)} %copy-done.29) | copy-start | bytes 1156
  745.1 130.9 %copy-start.26 = (f32[512]{0:T(512)S(1)}, f32[512]{0:T(512)}, u32[]{:S(2)}) copy-start(f32[512]{0:T(512)} %get-tuple-element.39) | copy-start | bytes 6148
  745.1 132.8 %copy-start.1 = (f32[367,1536]{1,0:T(8,128)S(1)}, f32[367,1536]{1,0:T(8,128)}, u32[]{:S(2)}) copy-start(f32[367,1536]{1,0:T(8,128)} %param.13) | copy-start | bytes 6764548
  (15 other events, 49.0 us)
Sparse Core Ops, SparseCore 0:
  383.4 73.2 reduce-scatter.3
  459.0 43.9 all-gather.7
  505.1 43.9 all-gather.5
  552.7 73.8 reduce-scatter.5
  628.7 43.9 all-gather.3
  677.7 67.3 all-reduce.3
  748.3 73.9 reduce-scatter.7
